TPU v7x, 256 devices: a whole 4x4x8 slice. The times are simulated.
256 devices in a mesh: leaf: 16 (over z, core), list: 16 (over y, x).
Axes of the slice: x: 4, y: 4, z: 8, core: 2. Of those that a mesh axis runs over, the one named last changes fastest.
Arguments:
- panel_charges: bfloat16 [4096, 64, 256], P(('leaf', 'list')), may hold values from -6 to 6
- leaf_basis: bfloat16 [4096, 64, 256], P(('leaf', 'list')), may hold values from -0.375 to 0.375
- near_blocks: bfloat16 [4096, 4, 256, 256], P(('leaf', 'list')), may hold values from -0.1875 to 0.1875
- near_list: int32 [4096, 4], P(('leaf', 'list')), may hold values from 0 to 15, as said below
- far_list: int32 [4096, 8], P(('leaf', 'list')), may hold values from 0 to 255, as said below
- far_count: int32 [4096], P(('leaf', 'list')), may hold values from 1 to 8, as said below
- far_coupling: bfloat16 [4096, 8, 64, 64], P(('leaf', 'list')), may hold values from -0.25 to 0.25
- leaf_transfer: float32 [4096, 64, 64], P(('leaf', 'list')), may hold values from -0.4375 to 0.4375
- device_transfer: float32 [16, 16, 64, 64], P('leaf', 'list'), may hold values from -0.375 to 0.375
- tree_transfer: float32 [24, 64, 64], replicated, may hold values from -0.75 to 0.75
- level_coupling: float32 [28, 4, 64, 64], replicated, may hold values from -0.4375 to 0.4375
Outputs:
- potential: bfloat16 [4096, 64, 256], P(('leaf', 'list'))
Inputs may be any that keep to these rules, and one draw needn't show every extreme that they name: `far_list`: each row names 8 different leaves of the leaf's group subtree, none on the leaf's own device; the 16 leaves of one device name, over all their slots, exactly 8 different leaves of each other device of the group. Slots at and after far_count[c] are unused. `near_list`: each row names 4 different leaves of the leaf's own device, the first being the leaf itself.
All inputs are finite; a program needn't handle non-finite values.
Results may differ from a plain program's by a relative error of at most 0.0053.
Values may be sent and summed in bfloat16 or wider, within the bound.
A program may use at most 64 MiB of HBM per device.

v0:
```python
import jax
import jax.numpy as jnp
from jax import lax
from jax.sharding import PartitionSpec as P

highest = lax.Precision.HIGHEST
offsets = (-3, -2, 2, 3)


def partner(array, axis, distance):
    return lax.ppermute(array, axis, [(i, i ^ 1 << distance) for i in range(lax.axis_size(axis))])


def shifted(array, axis, by):
    length = lax.axis_size(axis)
    pairs = [(i, i + by) for i in range(length) if 0 <= i + by < length]
    return lax.ppermute(array, axis, pairs)


def pick_usable(offset, parity):
    if offset == 3:
        return parity == 0
    if offset == -3:
        return parity == 1
    return parity >= 0


def upper_exchange(group_node, tree_transfer, level_coupling):
    leaf_count = lax.axis_size("leaf")
    depth = leaf_count.bit_length() - 2
    position = lax.axis_index("leaf")
    nodes = [group_node]
    for height in range(depth - 1):
        begin_row = 2 * leaf_count - 2 * (leaf_count >> height)
        matrix = tree_transfer[begin_row + (position >> height)]
        own_part = jnp.dot(nodes[-1], matrix, precision=highest)
        nodes.append(own_part + partner(own_part, "leaf", height))
    coupled = []
    for height in range(depth):
        begin_row = 2 * leaf_count - 2 * (leaf_count >> height)
        matrices = level_coupling[begin_row + (position >> height)]
        parity = (position >> height) % 2
        summed = jnp.zeros_like(group_node)
        for slot_index, offset in enumerate(offsets):
            source = shifted(nodes[height], "leaf", -offset * (1 << height))
            contribution = jnp.dot(source, matrices[slot_index].T, precision=highest)
            summed = summed + jnp.where(
                pick_usable(offset, parity), contribution, jnp.zeros((), jnp.float32)
            )
        coupled.append(summed)
    result = coupled[-1]
    for height in reversed(range(depth - 1)):
        begin_row = 2 * leaf_count - 2 * (leaf_count >> height)
        matrix = tree_transfer[begin_row + (position >> height)]
        result = coupled[height] + jnp.dot(result, matrix.T, precision=highest)
    return result


def on_device(
    panel_charges,
    leaf_basis,
    near_blocks,
    near_list,
    far_list,
    far_count,
    far_coupling,
    leaf_transfer,
    device_transfer,
    tree_transfer,
    level_coupling,
):
    leaf_local = panel_charges.shape[0]
    far_slots = far_list.shape[1]
    near_slots = near_list.shape[1]
    skeleton = jnp.einsum(
        "crm,ckm->crk", panel_charges, leaf_basis, preferred_element_type=jnp.float32
    ).astype(jnp.bfloat16)
    device_node = jnp.einsum(
        "irb,iba->ra", skeleton.astype(jnp.float32), leaf_transfer, precision=highest
    )
    device_term = jnp.dot(device_node, device_transfer[0, 0], precision=highest)
    group_node = lax.psum(device_term, "list")
    top_down = upper_exchange(group_node, tree_transfer, level_coupling)
    device_down = jnp.dot(top_down, device_transfer[0, 0].T, precision=highest)
    from_above = jnp.einsum("rd,ild->irl", device_down, leaf_transfer, precision=highest)
    row_width = skeleton.shape[1] * skeleton.shape[2]
    flattened = skeleton.reshape(leaf_local, row_width)
    wanted = far_list.reshape(-1)
    usable = (jnp.arange(far_slots, dtype=jnp.int32)[None, :] < far_count[:, None]).reshape(-1)
    piece = lax.all_gather(flattened, "list", axis=0, tiled=True)
    columns = jnp.arange(piece.shape[0], dtype=jnp.int32)
    hits = ((wanted[:, None] == columns[None, :]) & usable[:, None]).astype(jnp.bfloat16)
    collected = jnp.dot(hits, piece, preferred_element_type=jnp.float32)
    selected = collected.astype(jnp.bfloat16)
    selected = selected.reshape(leaf_local, far_slots, skeleton.shape[1], skeleton.shape[2])
    leaf_coupled = jnp.einsum(
        "ckrb,ckab->cra", selected, far_coupling, preferred_element_type=jnp.float32
    )
    coefficients = (leaf_coupled + from_above).astype(jnp.bfloat16)
    far_field = jnp.einsum(
        "crk,ckm->crm", coefficients, leaf_basis, preferred_element_type=jnp.float32
    )
    neighbours = jnp.take(panel_charges, near_list.reshape(-1), axis=0)
    neighbours = neighbours.reshape(
        leaf_local, near_slots, panel_charges.shape[1], panel_charges.shape[2]
    )
    near_field = jnp.einsum(
        "ckrm,cknm->crn", neighbours, near_blocks, preferred_element_type=jnp.float32
    )
    return (far_field + near_field).astype(jnp.bfloat16)


def solution(mesh):
    in_specs = (
        P(("leaf", "list"), None, None),
        P(("leaf", "list"), None, None),
        P(("leaf", "list"), None, None, None),
        P(("leaf", "list"), None),
        P(("leaf", "list"), None),
        P(("leaf", "list")),
        P(("leaf", "list"), None, None, None),
        P(("leaf", "list"), None, None),
        P("leaf", "list", None, None),
        P(),
        P(),
    )
    out_specs = P(("leaf", "list"), None, None)
    return jax.shard_map(
        on_device, mesh=mesh, in_specs=in_specs, out_specs=out_specs, check_vma=False
    )
```

profile of v0, /device:TPU:32, one launch (start us, length us, event | category | flops | bytes accessed | tf_op | source)
XLA Modules:
  0.0 177.3 jit_solution(7116425798900764517)
XLA Ops:
  6.5 1.6 convolution_convert_fusion.1
  8.2 1.4 convolution_bitcast_fusion.3
  10.5 74.6 %psum.7 = f32[64,64]{1,0:T(8,128)S(1)} all-reduce(f32[64,64]{1,0:T(8,128)S(1)} %fusion.34), channel_id=1, replica_groups=mesh['leaf'=16,'list'=16] {'list'}, use_global_device_ids=true, to_apply=%region_0.0 | all-reduce | flops 4096 | bytes 32768 | tf_op jit(solution)/shard_map/psum | solution.py:82
  85.1 1.3 collective-permute-start.3
  86.4 2.0 %collective-permute-start.2 = (f32[64,64]{1,0:T(8,128)S(1)}, f32[64,64]{1,0:T(8,128)S(1)}, u32[]{:S(2)}, u32[]{:S(2)}) collective-permute-start(f32[64,64]{1,0:T(8,128)S(1)} %psum.7), channel_id=1, source_target_pairs={{32,0},{48,16},{64,32},{80,48},{96,64},{112,80},{128,96},{144,112}... | collective-permute-start | bytes 49160 | tf_op jit(solution)/shard_map/ppermute | solution.py:17
  88.5 4.3 %collective-permute-start.1 = (f32[64,64]{1,0:T(8,128)S(1)}, f32[64,64]{1,0:T(8,128)S(1)}, u32[]{:S(2)}, u32[]{:S(2)}) collective-permute-start(f32[64,64]{1,0:T(8,128)S(1)} %psum.7), channel_id=1, source_target_pairs={{0,32},{16,48},{32,64},{48,80},{64,96},{80,112},{96,128},{112,144}... | collective-permute-start | bytes 49160 | tf_op jit(solution)/shard_map/ppermute | solution.py:17
  92.8 3.4 %collective-permute-start = (f32[64,64]{1,0:T(8,128)S(1)}, f32[64,64]{1,0:T(8,128)S(1)}, u32[]{:S(2)}, u32[]{:S(2)}) collective-permute-start(f32[64,64]{1,0:T(8,128)S(1)} %psum.7), channel_id=1, source_target_pairs={{0,48},{16,64},{32,80},{48,96},{64,112},{80,128},{96,144},{112,160... | collective-permute-start | bytes 49160 | tf_op jit(solution)/shard_map/ppermute | solution.py:17
  98.1 3.3 %collective-permute-start.4 = (f32[64,64]{1,0:T(8,128)S(1)}, f32[64,64]{1,0:T(8,128)S(1)}, u32[]{:S(2)}, u32[]{:S(2)}) collective-permute-start(f32[64,64]{1,0:T(8,128)S(1)} %fusion.31), channel_id=1, source_target_pairs={{0,16},{16,0},{32,48},{48,32},{64,80},{80,64},{96,112},{112,96},{1... | collective-permute-start | bytes 49160 | tf_op jit(solution)/shard_map/ppermute | solution.py:11
  103.1 2.0 %gather_fusion = bf16[64,64,256]{2,1,0:T(8,128)(2,1)} fusion(bf16[16,64,256]{2,1,0:T(8,128)(2,1)S(1)} %copy-done.1, s32[1024]{0:T(1024)S(1)} %pad_clamp_fusion), kind=kCustom, calls=%fused_computation | custom fusion | bytes 4194560 | tf_op jit(solution)/shard_map/jit(_take)/gather | solution.py:103
  105.1 6.8 %fusion.3 = f32[16,64,256]{2,1,0:T(8,128)S(1)} fusion(bf16[16,4,256,256]{3,2,1,0:T(8,128)(2,1)} %param.13, bf16[16,4,64,256]{3,2,1,0:T(8,128)(2,1)} %bitcast.100, pred[16,4]{1,0:T(8,128)(4,1)S(1)} %copy.16), kind=kOutput, calls=%fused_computation.5 | convolution fusion | flops 537919488 | bytes 11534400 | tf_op jit(solution)/shard_map/ckrm,cknm->crn/dot_general | solution.py:107
  112.3 1.3 collective-permute-start.8
  114.5 1.3 collective-permute-start.7
  116.8 5.5 %collective-permute-start.6 = (f32[64,64]{1,0:T(8,128)S(1)}, f32[64,64]{1,0:T(8,128)S(1)}, u32[]{:S(2)}, u32[]{:S(2)}) collective-permute-start(f32[64,64]{1,0:T(8,128)S(1)} %add.117), channel_id=1, source_target_pairs={{0,64},{16,80},{32,96},{48,112},{64,128},{80,144},{96,160},{112,17... | collective-permute-start | bytes 49160 | tf_op jit(solution)/shard_map/ppermute | solution.py:17
  124.7 2.6 %collective-permute-done.9 = f32[64,64]{1,0:T(8,128)S(1)} collective-permute-done((f32[64,64]{1,0:T(8,128)S(1)}, f32[64,64]{1,0:T(8,128)S(1)}, u32[]{:S(2)}, u32[]{:S(2)}) %collective-permute-start.9) | collective-permute-done | bytes 16416 | tf_op jit(solution)/shard_map/ppermute | solution.py:11
  127.3 7.4 %collective-permute-start.5 = (f32[64,64]{1,0:T(8,128)S(1)}, f32[64,64]{1,0:T(8,128)S(1)}, u32[]{:S(2)}, u32[]{:S(2)}) collective-permute-start(f32[64,64]{1,0:T(8,128)S(1)} %add.117), channel_id=1, source_target_pairs={{0,96},{16,112},{32,128},{48,144},{64,160},{80,176},{96,192},{112,... | collective-permute-start | bytes 49160 | tf_op jit(solution)/shard_map/ppermute | solution.py:17
  134.8 1.3 collective-permute-start.13
  136.1 0.9 convolution_select_fusion.5
  137.1 1.3 collective-permute-start.12
  138.4 1.0 convolution_select_fusion.6
  139.3 8.5 %collective-permute-start.11 = (f32[64,64]{1,0:T(8,128)S(1)}, f32[64,64]{1,0:T(8,128)S(1)}, u32[]{:S(2)}, u32[]{:S(2)}) collective-permute-start(f32[64,64]{1,0:T(8,128)S(1)} %add.125), channel_id=1, source_target_pairs={{0,128},{16,144},{32,160},{48,176},{64,192},{80,208},{96,224},{112... | collective-permute-start | bytes 49160 | tf_op jit(solution)/shard_map/ppermute | solution.py:17
  148.8 1.3 collective-permute-start.10
  150.1 1.0 convolution_select_fusion.1
  151.0 1.0 convolution_select_fusion.2
  152.0 1.0 convolution_select_fusion
  153.0 1.0 fusion.11
  154.9 1.0 fusion.15
  156.8 1.0 fusion.19
  158.0 3.1 %convolution_convert_fusion = bf16[128,4096]{1,0:T(8,128)(2,1)} fusion(bf16[256,4096]{1,0:T(8,128)(2,1)} %all-gather.2.cloned.1.call-done, s32[128]{0:T(128)S(1)} %eq.37, pred[128]{0:T(512)(128)(4,1)S(1)} %lt.70), kind=kOutput, calls=%fused_computation.1 | convolution fusion | flops 269025280 | bytes 3146368 | tf_op jit(solution)/shard_map/dot_general | solution.py:93
  161.1 4.3 %reshape.87 = bf16[16,8,64,64]{3,2,1,0:T(8,128)(2,1)} reshape(bf16[128,4096]{1,0:T(8,128)(2,1)} %convolution_convert_fusion) | data formatting | bytes 2097152 | tf_op jit(solution)/shard_map/reshape | solution.py:95
  165.3 2.4 %convolution_bitcast_fusion = f32[16,64,64]{2,1,0:T(8,128)S(1)} fusion(bf16[16,8,64,64]{3,2,1,0:T(8,128)(2,1)} %reshape.87, bf16[16,8,64,64]{3,2,1,0:T(8,128)(2,1)S(1)} %copy-done), kind=kOutput, calls=%fused_computation.8 | convolution fusion | flops 67108864 | bytes 2359296 | tf_op jit(solution)/shard_map/ckrb,ckab->cra/dot_general | solution.py:96
  167.7 1.6 fusion.8
  169.3 1.1 fusion.6
  (54 shorter events, 12.1 us)
Async XLA Ops:
  6.5 158.8 %copy-start = (bf16[16,8,64,64]{3,2,1,0:T(8,128)(2,1)S(1)}, bf16[16,8,64,64]{3,2,1,0:T(8,128)(2,1)}, u32[]{:S(2)}) copy-start(bf16[16,8,64,64]{3,2,1,0:T(8,128)(2,1)} %param.17) | copy-start | bytes 3145732
  6.5 96.5 %copy-start.1 = (bf16[16,64,256]{2,1,0:T(8,128)(2,1)S(1)}, bf16[16,64,256]{2,1,0:T(8,128)(2,1)}, u32[]{:S(2)}) copy-start(bf16[16,64,256]{2,1,0:T(8,128)(2,1)} %param.11) | copy-start | bytes 1572868
  6.5 151.5 %all-gather.2.cloned.1.call-start = ((), (), s32[]{:S(2)}) async-start(), calls=%async_computation | async-start | bytes 2228224 | tf_op jit(solution)/shard_map/all_gather | solution.py:90
  85.1 38.2 %collective-permute-start.3 = (f32[64,64]{1,0:T(8,128)S(1)}, f32[64,64]{1,0:T(8,128)S(1)}, u32[]{:S(2)}, u32[]{:S(2)}) collective-permute-start(f32[64,64]{1,0:T(8,128)S(1)} %psum.7), channel_id=1, source_target_pairs={{48,0},{64,16},{80,32},{96,48},{112,64},{128,80},{144,96},{160,112... | collective-permute-start | bytes 49160 | tf_op jit(solution)/shard_map/ppermute | solution.py:17
  86.4 28.1 %collective-permute-start.2 = (f32[64,64]{1,0:T(8,128)S(1)}, f32[64,64]{1,0:T(8,128)S(1)}, u32[]{:S(2)}, u32[]{:S(2)}) collective-permute-start(f32[64,64]{1,0:T(8,128)S(1)} %psum.7), channel_id=1, source_target_pairs={{32,0},{48,16},{64,32},{80,48},{96,64},{112,80},{128,96},{144,112}... | collective-permute-start | bytes 49160 | tf_op jit(solution)/shard_map/ppermute | solution.py:17
  88.5 28.3 %collective-permute-start.1 = (f32[64,64]{1,0:T(8,128)S(1)}, f32[64,64]{1,0:T(8,128)S(1)}, u32[]{:S(2)}, u32[]{:S(2)}) collective-permute-start(f32[64,64]{1,0:T(8,128)S(1)} %psum.7), channel_id=1, source_target_pairs={{0,32},{16,48},{32,64},{48,80},{64,96},{80,112},{96,128},{112,144}... | collective-permute-start | bytes 49160 | tf_op jit(solution)/shard_map/ppermute | solution.py:17
  92.8 64.0 %collective-permute-start = (f32[64,64]{1,0:T(8,128)S(1)}, f32[64,64]{1,0:T(8,128)S(1)}, u32[]{:S(2)}, u32[]{:S(2)}) collective-permute-start(f32[64,64]{1,0:T(8,128)S(1)} %psum.7), channel_id=1, source_target_pairs={{0,48},{16,64},{32,80},{48,96},{64,112},{80,128},{96,144},{112,160... | collective-permute-start | bytes 49160 | tf_op jit(solution)/shard_map/ppermute | solution.py:17
  98.1 14.2 %collective-permute-start.4 = (f32[64,64]{1,0:T(8,128)S(1)}, f32[64,64]{1,0:T(8,128)S(1)}, u32[]{:S(2)}, u32[]{:S(2)}) collective-permute-start(f32[64,64]{1,0:T(8,128)S(1)} %fusion.31), channel_id=1, source_target_pairs={{0,16},{16,0},{32,48},{48,32},{64,80},{80,64},{96,112},{112,96},{1... | collective-permute-start | bytes 49160 | tf_op jit(solution)/shard_map/ppermute | solution.py:11
  105.1 6.9 %copy-start.6 = (s32[16]{0:T(128)S(1)}, s32[16]{0:T(128)}, u32[]{:S(2)}) copy-start(s32[16]{0:T(128)} %param.16) | copy-start | bytes 196
  105.1 7.0 %copy-start.5 = (s32[16,8]{0,1:T(8,128)S(1)}, s32[16,8]{0,1:T(8,128)}, u32[]{:S(2)}) copy-start(s32[16,8]{0,1:T(8,128)} %param.15) | copy-start | bytes 1540
  105.1 52.7 %copy-start.4 = (f32[1,1,64,64]{3,2,1,0:T(8,128)S(1)}, f32[1,1,64,64]{3,2,1,0:T(8,128)}, u32[]{:S(2)}) copy-start(f32[1,1,64,64]{3,2,1,0:T(8,128)} %param.19) | copy-start | bytes 49156
  112.3 27.0 %collective-permute-start.8 = (f32[64,64]{1,0:T(8,128)S(1)}, f32[64,64]{1,0:T(8,128)S(1)}, u32[]{:S(2)}, u32[]{:S(2)}) collective-permute-start(f32[64,64]{1,0:T(8,128)S(1)} %add.117), channel_id=1, source_target_pairs={{96,0},{112,16},{128,32},{144,48},{160,64},{176,80},{192,96},{208,... | collective-permute-start | bytes 49160 | tf_op jit(solution)/shard_map/ppermute | solution.py:17
  114.5 20.3 %collective-permute-start.7 = (f32[64,64]{1,0:T(8,128)S(1)}, f32[64,64]{1,0:T(8,128)S(1)}, u32[]{:S(2)}, u32[]{:S(2)}) collective-permute-start(f32[64,64]{1,0:T(8,128)S(1)} %add.117), channel_id=1, source_target_pairs={{64,0},{80,16},{96,32},{112,48},{128,64},{144,80},{160,96},{176,11... | collective-permute-start | bytes 49160 | tf_op jit(solution)/shard_map/ppermute | solution.py:17
  116.8 20.3 %collective-permute-start.6 = (f32[64,64]{1,0:T(8,128)S(1)}, f32[64,64]{1,0:T(8,128)S(1)}, u32[]{:S(2)}, u32[]{:S(2)}) collective-permute-start(f32[64,64]{1,0:T(8,128)S(1)} %add.117), channel_id=1, source_target_pairs={{0,64},{16,80},{32,96},{48,112},{64,128},{80,144},{96,160},{112,17... | collective-permute-start | bytes 49160 | tf_op jit(solution)/shard_map/ppermute | solution.py:17
  123.3 4.0 %collective-permute-start.9 = (f32[64,64]{1,0:T(8,128)S(1)}, f32[64,64]{1,0:T(8,128)S(1)}, u32[]{:S(2)}, u32[]{:S(2)}) collective-permute-start(f32[64,64]{1,0:T(8,128)S(1)} %fusion.27), channel_id=1, source_target_pairs={{0,32},{16,48},{32,0},{48,16},{64,96},{80,112},{96,64},{112,80},{1... | collective-permute-start | bytes 49160 | tf_op jit(solution)/shard_map/ppermute | solution.py:11
  127.3 27.6 %collective-permute-start.5 = (f32[64,64]{1,0:T(8,128)S(1)}, f32[64,64]{1,0:T(8,128)S(1)}, u32[]{:S(2)}, u32[]{:S(2)}) collective-permute-start(f32[64,64]{1,0:T(8,128)S(1)} %add.117), channel_id=1, source_target_pairs={{0,96},{16,112},{32,128},{48,144},{64,160},{80,176},{96,192},{112,... | collective-permute-start | bytes 49160 | tf_op jit(solution)/shard_map/ppermute | solution.py:17
  134.8 17.2 %collective-permute-start.13 = (f32[64,64]{1,0:T(8,128)S(1)}, f32[64,64]{1,0:T(8,128)S(1)}, u32[]{:S(2)}, u32[]{:S(2)}) collective-permute-start(f32[64,64]{1,0:T(8,128)S(1)} %add.125), channel_id=1, source_target_pairs={{192,0},{208,16},{224,32},{240,48},{193,1},{209,17},{225,33},{241,... | collective-permute-start | bytes 49160 | tf_op jit(solution)/shard_map/ppermute | solution.py:17
  137.1 11.7 %collective-permute-start.12 = (f32[64,64]{1,0:T(8,128)S(1)}, f32[64,64]{1,0:T(8,128)S(1)}, u32[]{:S(2)}, u32[]{:S(2)}) collective-permute-start(f32[64,64]{1,0:T(8,128)S(1)} %add.125), channel_id=1, source_target_pairs={{128,0},{144,16},{160,32},{176,48},{192,64},{208,80},{224,96},{240... | collective-permute-start | bytes 49160 | tf_op jit(solution)/shard_map/ppermute | solution.py:17
  139.3 11.7 %collective-permute-start.11 = (f32[64,64]{1,0:T(8,128)S(1)}, f32[64,64]{1,0:T(8,128)S(1)}, u32[]{:S(2)}, u32[]{:S(2)}) collective-permute-start(f32[64,64]{1,0:T(8,128)S(1)} %add.125), channel_id=1, source_target_pairs={{0,128},{16,144},{32,160},{48,176},{64,192},{80,208},{96,224},{112... | collective-permute-start | bytes 49160 | tf_op jit(solution)/shard_map/ppermute | solution.py:17
  148.8 4.2 %collective-permute-start.10 = (f32[64,64]{1,0:T(8,128)S(1)}, f32[64,64]{1,0:T(8,128)S(1)}, u32[]{:S(2)}, u32[]{:S(2)}) collective-permute-start(f32[64,64]{1,0:T(8,128)S(1)} %add.125), channel_id=1, source_target_pairs={{0,192},{16,208},{32,224},{48,240},{1,193},{17,209},{33,225},{49,2... | collective-permute-start | bytes 49160 | tf_op jit(solution)/shard_map/ppermute | solution.py:17
  165.3 2.4 %copy-start.2 = (f32[16,64,64]{2,1,0:T(8,128)S(1)}, f32[16,64,64]{2,1,0:T(8,128)}, u32[]{:S(2)}) copy-start(f32[16,64,64]{2,1,0:T(8,128)} %param.18) | copy-start | bytes 786436
  165.3 4.0 %copy-start.3 = (bf16[16,64,256]{2,1,0:T(8,128)(2,1)S(1)}, bf16[16,64,256]{2,1,0:T(8,128)(2,1)}, u32[]{:S(2)}) copy-start(bf16[16,64,256]{2,1,0:T(8,128)(2,1)} %param.12) | copy-start | bytes 1572868
Sparse Core Ops, SparseCore 0:
  97.3 47.2 all-gather.1
where the time goes:
time: 179 us; the launch traced here: 177 us
  blocking collectives  74.6 us (42%)
  starting transfers between devices  42.7 us (24%)
  matrix products  34.2 us (19%)
  between operations  13.8 us (8%)
  local copies, waits for them, and re-layouts  8.41 us (5%)
  waiting for transfers between devices  2.66 us (1%)
    psum x1, blocking collectives, on_device(): group_node = lax.psum(device_term, 'list')  74.6 us
    ppermute x12, starting transfers between devices, shifted(): return lax.ppermute(array, axis, pairs)  38.9 us
    dot_general x12, matrix products, upper_exchange(): contribution = jnp.dot(source, matrices[slot_index].T, precision=highest)  11.4 us
    dot_general x1, matrix products, on_device(): jnp.einsum('ckrm,cknm->crn', neighbours, near_blocks, preferred_element_t...  6.84 us
    reshape x1, local copies, waits for them, and re-layouts, on_device(): selected.reshape(leaf_local, far_slots, skeleton.shape[1], skeleton.shape...  4.26 us
    ppermute x2, starting transfers between devices, partner(): lax.ppermute(array, axis, [(i, i ^ 1 << distance) for i in range(lax.axis...  3.79 us
  transfers between devices with their start and end apart: 15, of which 1 were waited for; matrix products, arithmetic and copies ran while one was open for 15% of the time, Pallas kernels for 0%

commit v1 on v0

v1 whole, which is shorter than its diff:
```python
import jax
import jax.numpy as jnp
from jax import lax
from jax.experimental import pallas as pl
from jax.experimental.pallas import tpu as pltpu
from jax.sharding import PartitionSpec as P

MESH = pl.DeviceIdType.MESH
f32, bf16, i32 = jnp.float32, jnp.bfloat16, jnp.int32
SIDE = 4
LIST = 16
LEAF = 16
LEAVES = 16
PAIRS = LEAVES // 2
R = 64
K = 64
M = 256
NFAR = 8
NNEAR = 4
HALF = PAIRS // 2
DEEP = NFAR * 128 + 256
offsets = (-3, -2, 2, 3)
NT = (((1,), (1,)), ((), ()))


def messages():
    q = HALF // 2
    table = [
        ((1, 0), (0, 0), 0, HALF),
        ((-1, 0), (0, 0), 0, HALF),
        ((1, 0), (-1, 0), 0, q),
        ((-1, 0), (1, 0), q, q),
    ]
    for block, begin, count in ((0, 0, HALF), (-1, 0, HALF), (1, 0, HALF), (2, 0, q), (2, q, q)):
        table.append(((0, 1), (block, 0), begin, count))
        table.append(((0, -1), (block, 0), begin, count))
    for block in (0, -1, 1, 2):
        table.append(((0, 1), (block, -1), 0, q))
        table.append(((0, -1), (block, 1), q, q))
    return table


TABLE = messages()
COPIES = len(TABLE)


def split(x):
    high = x.astype(bf16)
    return high, (x - high.astype(f32)).astype(bf16)


def left_half(shape):
    return lax.broadcasted_iota(i32, shape, len(shape) - 1) % 128 < 64


def swap(x):
    return pltpu.roll(x, 64, x.ndim - 1)


def level_of(a, b):
    near_parents = jnp.abs(a // 2 - b // 2) <= 1
    near_grand = jnp.abs(a // 4 - b // 4) <= 1
    return jnp.where(near_parents, 0, jnp.where(near_grand, 1, 2))


def kernel(
    charges_hbm, basis_hbm, near_hbm, nlist_hbm, flist_hbm, fcount_hbm, coup_hbm, lt_hbm, dt_hbm, tt_hbm, lc_hbm,
    out_hbm,
    charges, basis, near, nlist, flist, fcount, coup, lt, dt, tt, lc,
    skel, gup, deep, acc, wtab, wcat, ubd, tsend, rs, zsend, zrecv, ag, out,
    load_sem, near_sem, coup_sem, out_sem, skel_send, skel_recv, rs_send, rs_recv, z_send, z_recv, ag_send, ag_recv,
):
    l = lax.axis_index("leaf")
    j = lax.axis_index("list")
    x, y = j % SIDE, j // SIDE

    loads = [
        pltpu.make_async_copy(charges_hbm, charges, load_sem.at[0]),
        pltpu.make_async_copy(basis_hbm, basis, load_sem.at[1]),
        pltpu.make_async_copy(lt_hbm, lt, load_sem.at[2]),
        pltpu.make_async_copy(dt_hbm.at[0, 0], dt, load_sem.at[3]),
        pltpu.make_async_copy(nlist_hbm, nlist, load_sem.at[4]),
        pltpu.make_async_copy(flist_hbm, flist, load_sem.at[5]),
        pltpu.make_async_copy(fcount_hbm, fcount, load_sem.at[6]),
        pltpu.make_async_copy(tt_hbm.at[l], tt.at[0], load_sem.at[7]),
        pltpu.make_async_copy(tt_hbm.at[LEAF + l // 2], tt.at[1], load_sem.at[8]),
        pltpu.make_async_copy(lc_hbm.at[l], lc.at[0], load_sem.at[9]),
        pltpu.make_async_copy(lc_hbm.at[LEAF + l // 2], lc.at[1], load_sem.at[10]),
        pltpu.make_async_copy(lc_hbm.at[LEAF + LEAF // 2 + l // 4], lc.at[2], load_sem.at[11]),
    ]
    for load in loads:
        load.start()

    def near_copy(c):
        return pltpu.make_async_copy(near_hbm.at[c], near.at[c], near_sem.at[c])

    def coup_copy(c):
        return pltpu.make_async_copy(coup_hbm.at[c], coup.at[c], coup_sem.at[c])

    def out_copy(c):
        return pltpu.make_async_copy(out.at[c], out_hbm.at[c], out_sem.at[c])

    barrier = pltpu.get_barrier_semaphore()

    @pl.loop(1, LIST)
    def _(o):
        pl.semaphore_signal(barrier, inc=1, device_id={"list": (j + o) % LIST}, device_id_type=MESH)

    @pl.loop(1, LEAF)
    def _(o):
        pl.semaphore_signal(barrier, inc=1, device_id={"leaf": (l + o) % LEAF}, device_id_type=MESH)

    @pl.loop(0, LEAVES)
    def _(c):
        near_copy(c).start()
        coup_copy(c).start()

    loads[2].wait()
    loads[3].wait()
    twice = jnp.concatenate([dt[...], dt[...]], axis=1)
    g = jnp.dot(lt[...].reshape(LEAVES * K, K), twice, precision=lax.Precision.HIGHEST)
    g_high, g_low = split(g)
    wide = left_half((LEAVES * K, 128))
    high32, low32 = g_high.astype(f32), g_low.astype(f32)
    gup[...] = jnp.where(wide, high32, low32).astype(bf16)
    deep[:, :, NFAR * 128 : NFAR * 128 + 128] = g_high.reshape(LEAVES, K, 128)
    deep[:, :, NFAR * 128 + 128 :] = jnp.where(wide, low32, 0.0).astype(bf16).reshape(LEAVES, K, 128)

    loads[0].wait()
    loads[1].wait()
    for i in range(PAIRS):
        both = lax.dot_general(
            charges[2 * i : 2 * i + 2].reshape(2 * R, M),
            basis[2 * i : 2 * i + 2].reshape(2 * K, M),
            NT,
            preferred_element_type=f32,
        )
        skel[j * PAIRS + i] = jnp.where(left_half((R, 128)), both[:R], both[R:]).astype(bf16)

    own = jnp.concatenate([skel[j * PAIRS + i] for i in range(PAIRS)], axis=1)
    term = jnp.dot(own, gup[...], preferred_element_type=f32)
    term = term + swap(term)
    for group in range(SIDE):
        rows = term[16 * group : 16 * group + 16]
        tsend[group] = jnp.where(left_half((8, 128)), rows[:8], rows[8:])
    rs[j] = tsend[y]

    pl.semaphore_wait(barrier, LIST + LEAF - 2)

    def rs_copy(o):
        peer = (j + o) % LIST
        return pltpu.make_async_remote_copy(
            src_ref=tsend.at[peer // SIDE],
            dst_ref=rs.at[j],
            send_sem=rs_send.at[o],
            recv_sem=rs_recv.at[o],
            device_id={"list": peer},
            device_id_type=MESH,
        )

    def z_copy(o):
        peer = (l + o) % LEAF
        return pltpu.make_async_remote_copy(
            src_ref=zsend.at[level_of(l, peer)],
            dst_ref=zrecv.at[l],
            send_sem=z_send.at[o],
            recv_sem=z_recv.at[o],
            device_id={"leaf": peer},
            device_id_type=MESH,
        )

    def ag_copy(o):
        return pltpu.make_async_remote_copy(
            src_ref=ag.at[y],
            dst_ref=ag.at[y],
            send_sem=ag_send.at[o],
            recv_sem=ag_recv.at[o],
            device_id={"list": (y + o) % SIDE * SIDE + x},
            device_id_type=MESH,
        )

    def skel_copy(half, index):
        to, block, begin, count = TABLE[index]
        if half:
            to, block = to[::-1], block[::-1]

        def place(at):
            return (y + at[1] + SIDE) % SIDE * SIDE + (x + at[0] + SIDE) % SIDE

        where = skel.at[pl.ds(place(block) * PAIRS + half * HALF + begin, count)]
        return pltpu.make_async_remote_copy(
            src_ref=where,
            dst_ref=where,
            send_sem=skel_send.at[half, index],
            recv_sem=skel_recv.at[half, index],
            device_id={"list": place(to)},
            device_id_type=MESH,
        )

    def send(*indices):
        for index in indices:
            for half in (0, 1):
                skel_copy(half, index).start()

    def receive(*indices):
        for index in indices:
            for half in (0, 1):
                skel_copy(half, index).wait_recv()

    @pl.loop(1, LIST)
    def _(o):
        rs_copy(o).start()

    send(0, 1, 4, 5)

    for load in loads[4:]:
        load.wait()
    first = tt[0]
    second = jnp.dot(first, tt[1], precision=lax.Precision.HIGHEST)
    for h, u in enumerate((None, first, second)):
        for s in range(4):
            matrix = lc[h, s]
            doubled = jnp.concatenate([matrix, matrix], axis=1)
            if h:
                doubled = jnp.dot(u, doubled, precision=lax.Precision.HIGHEST)
            wtab[h * 4 + s] = doubled
    wtab[12] = jnp.zeros((K, 128), f32)

    def table_row(peer):
        h = level_of(l, peer)
        d = jnp.where(h == 0, peer - l, jnp.where(h == 1, peer // 2 - l // 2, peer // 4 - l // 4))
        slot = jnp.where(d < 0, d + 3, d)
        return jnp.where(jnp.abs(peer - l) >= 2, h * 4 + slot, 12)

    square = left_half((K, 128))
    for i in range(LEAF // 2):
        w = jnp.where(square, wtab[table_row(2 * i)], wtab[table_row(2 * i + 1)])
        high, low = split(w)
        wcat[:K, 128 * i : 128 * i + 128] = high
        wcat[K:, 128 * i : 128 * i + 128] = low
    for n, u in enumerate((first, second)):
        doubled = jnp.concatenate([u, u], axis=1)
        block = jnp.concatenate([jnp.where(square, doubled, 0.0), jnp.where(square, 0.0, doubled)], axis=0)
        high, low = split(block)
        ubd[:, 128 * n : 128 * n + 128] = high
        ubd[:, 256 + 128 * n : 256 + 128 * n + 128] = low
    zrecv[l] = jnp.zeros((8, 128), f32)

    def near_leaves(begin, end):
        @pl.loop(begin, end)
        def _(c):
            near_copy(c).wait()
            coup_copy(c).wait()
            total = lax.dot_general(charges[nlist[c, 0]], near[c, 0], NT, preferred_element_type=f32)
            for k in range(1, NNEAR):
                total += lax.dot_general(charges[nlist[c, k]], near[c, k], NT, preferred_element_type=f32)
            acc[c] = total
            for k in range(NFAR):
                matrix = coup[c, k]
                deep[c, :, 128 * k : 128 * k + 128] = jnp.concatenate([matrix, matrix], axis=1)

    near_leaves(0, 5)

    receive(0, 1)
    send(2, 3, 6, 7, 8, 9)
    receive(4, 5)
    send(14, 15)

    @pl.loop(1, LIST)
    def _(o):
        rs_copy(o).wait_recv()

    node = jnp.sum(rs[...], axis=0)
    high, low = split(node)
    product = jnp.dot(jnp.concatenate([high, low], axis=0), ubd[...], preferred_element_type=f32)
    product = product[:8] + product[8:]
    product = product[:, :256] + product[:, 256:]
    zsend[0] = node
    zsend[1] = product[:, :128]
    zsend[2] = product[:, 128:]

    @pl.loop(1, LEAF)
    def _(o):
        z_copy(o).start()

    near_leaves(5, 10)

    receive(2, 3)
    send(10, 11, 12, 13)
    receive(6, 7, 8, 9)
    send(16, 17, 18, 19)

    near_leaves(10, 14)

    @pl.loop(1, LEAF)
    def _(o):
        z_copy(o).wait_recv()

    tops, bottoms = [], []
    narrow = left_half((8, 128))
    for i in range(LEAF // 2):
        even, odd = zrecv[2 * i], zrecv[2 * i + 1]
        tops.append(jnp.where(narrow, even, swap(odd)))
        bottoms.append(jnp.where(narrow, swap(even), odd))
    nodes = jnp.concatenate([jnp.concatenate(tops, axis=1), jnp.concatenate(bottoms, axis=1)], axis=0)
    high, low = split(nodes)
    down = lax.dot_general(jnp.concatenate([high, low], axis=0), wcat[...], NT, preferred_element_type=f32)
    down = down[:16] + down[16:]
    down = down + swap(down)
    ag[y] = jnp.where(narrow, down[:8], down[8:])
    for o in range(1, SIDE):
        ag_copy(o).start()

    receive(10, 13)
    send(20, 21)

    near_leaves(14, 16)

    for o in range(1, SIDE):
        ag_copy(o).wait_recv()
    parts = []
    for group in range(SIDE):
        tile = ag[group]
        other = swap(tile)
        parts += [jnp.where(narrow, tile, other), jnp.where(narrow, other, tile)]
    top_down = jnp.concatenate(parts, axis=0)
    high = top_down.astype(bf16).astype(f32)
    above = jnp.concatenate(
        [
            jnp.where(square, high, top_down - high).astype(bf16),
            jnp.where(square, high, 0.0).astype(bf16),
        ],
        axis=1,
    )

    receive(11, 12, 14, 15, 16, 17, 18, 19, 20, 21)

    lane = lax.broadcasted_iota(i32, (1, 128), 1) // 64

    @pl.loop(0, LEAVES)
    def _(c):
        pieces = []
        for k in range(NFAR):
            source = flist[c, k]
            wanted = jnp.where(k < fcount[c], source % 2, 2)
            keep = jnp.where(lane == wanted, 1.0, 0.0).astype(bf16)
            pieces.append(skel[source // 2] * keep)
        pieces.append(above)
        coefficients = lax.dot_general(jnp.concatenate(pieces, axis=1), deep[c], NT, preferred_element_type=f32).astype(bf16)
        far = jnp.dot(coefficients, basis[c], preferred_element_type=f32)
        out[c] = (far + acc[c]).astype(bf16)
        out_copy(c).start()

    for index in range(COPIES):
        for half in (0, 1):
            skel_copy(half, index).wait_send()

    @pl.loop(1, LIST)
    def _(o):
        rs_copy(o).wait_send()

    @pl.loop(1, LEAF)
    def _(o):
        z_copy(o).wait_send()

    for o in range(1, SIDE):
        ag_copy(o).wait_send()

    @pl.loop(0, LEAVES)
    def _(c):
        out_copy(c).wait()


def on_device(*args):
    anywhere = pl.BlockSpec(memory_space=pl.ANY)
    dma = pltpu.SemaphoreType.DMA
    return pl.pallas_call(
        kernel,
        out_shape=jax.ShapeDtypeStruct((LEAVES, R, M), bf16),
        in_specs=[anywhere] * len(args),
        out_specs=anywhere,
        scratch_shapes=[
            pltpu.VMEM((LEAVES, R, M), bf16),
            pltpu.VMEM((LEAVES, K, M), bf16),
            pltpu.VMEM((LEAVES, NNEAR, M, M), bf16),
            pltpu.SMEM((LEAVES, NNEAR), i32),
            pltpu.SMEM((LEAVES, NFAR), i32),
            pltpu.SMEM((LEAVES,), i32),
            pltpu.VMEM((LEAVES, NFAR, K, K), bf16),
            pltpu.VMEM((LEAVES, K, K), f32),
            pltpu.VMEM((K, K), f32),
            pltpu.VMEM((2, K, K), f32),
            pltpu.VMEM((3, 4, K, K), f32),
            pltpu.VMEM((LIST * PAIRS, R, 128), bf16),
            pltpu.VMEM((LEAVES * K, 128), bf16),
            pltpu.VMEM((LEAVES, K, DEEP), bf16),
            pltpu.VMEM((LEAVES, R, M), f32),
            pltpu.VMEM((13, K, 128), f32),
            pltpu.VMEM((2 * K, LEAF * K), bf16),
            pltpu.VMEM((128, 512), bf16),
            pltpu.VMEM((SIDE, 8, 128), f32),
            pltpu.VMEM((LIST, 8, 128), f32),
            pltpu.VMEM((3, 8, 128), f32),
            pltpu.VMEM((LEAF, 8, 128), f32),
            pltpu.VMEM((SIDE, 8, 128), f32),
            pltpu.VMEM((LEAVES, R, M), bf16),
            dma((12,)),
            dma((LEAVES,)),
            dma((LEAVES,)),
            dma((LEAVES,)),
            dma((2, COPIES)),
            dma((2, COPIES)),
            dma((LIST,)),
            dma((LIST,)),
            dma((LEAF,)),
            dma((LEAF,)),
            dma((SIDE,)),
            dma((SIDE,)),
        ],
        compiler_params=pltpu.CompilerParams(collective_id=0, has_side_effects=True),
        name="h2_product",
    )(*args)


def solution(mesh):
    in_specs = (
        P(("leaf", "list"), None, None),
        P(("leaf", "list"), None, None),
        P(("leaf", "list"), None, None, None),
        P(("leaf", "list"), None),
        P(("leaf", "list"), None),
        P(("leaf", "list")),
        P(("leaf", "list"), None, None, None),
        P(("leaf", "list"), None, None),
        P("leaf", "list", None, None),
        P(),
        P(),
    )
    out_specs = P(("leaf", "list"), None, None)
    return jax.shard_map(on_device, mesh=mesh, in_specs=in_specs, out_specs=out_specs, check_vma=False)
```

time: 179 us -> 38.6 us (0.22)
  blocking collectives: 74.6 us -> 0 us
  starting transfers between devices: 42.7 us -> 0 us
  matrix products: 34.2 us -> 0 us
  Pallas kernels: 0 us -> 33.6 us
  between operations: 13.8 us -> 0.01 us
  local copies, waits for them, and re-layouts: 8.41 us -> 4.58 us
  waiting for transfers between devices: 2.66 us -> 0 us
    psum x1 -> x0, blocking collectives: 74.6 us -> none  [on_device(): group_node = lax.psum(device_term, 'list')]
    ppermute x14 -> x0, starting transfers between devices: 42.7 us -> none  [the longest x12 38.9 us: shifted(): return lax.ppermute(array, axis, pairs)]
    dot_general x25 -> x0, matrix products: 34.2 us -> none  [the longest x12 11.4 us: upper_exchange(): contribution = jnp.dot(source, matrices[slot_index].T, precision=highest)]
    pallas_call x0 -> x1, Pallas kernels: none -> 33.6 us  [on_device(): pl.pallas_call(kernel, out_shape=jax.ShapeDtypeStruct((LEAVES, R, M), bf1...]
    reshape x3 -> x0, local copies, waits for them, and re-layouts: 5.27 us -> none  [the longest x1 4.26 us: on_device(): selected.reshape(leaf_local, far_slots, skeleton.shape[1], skeleton.shape...]
    unnamed x16 -> x3, local copies, waits for them, and re-layouts: 0.87 us -> 4.58 us
    ppermute x14 -> x0, waiting for transfers between devices: 2.63 us -> none  [the longest x2 2.6 us: partner(): lax.ppermute(array, axis, [(i, i ^ 1 << distance) for i in range(lax.axis...]
    gather x1 -> x0, local copies, waits for them, and re-layouts: 1.99 us -> none  [on_device(): neighbours = jnp.take(panel_charges, near_list.reshape(-1), axis=0)]
  transfers between devices with their start and end apart: 15 -> 0, of which waited for: 1 -> 0; matrix products, arithmetic and copies ran while one was open for 15% -> 0% of each run, Pallas kernels for 0% -> 0%
where the time goes in v1:
time: 38.6 us; the launch traced here: 38.2 us
  Pallas kernels  33.6 us (87%)
  local copies, waits for them, and re-layouts  4.58 us (12%)
    pallas_call x1, Pallas kernels, on_device(): pl.pallas_call(kernel, out_shape=jax.ShapeDtypeStruct((LEAVES, R, M), bf1...  33.6 us
    unnamed x3, local copies, waits for them, and re-layouts  4.58 us

profile of v1, /device:TPU:32, one launch (start us, length us, event | category | flops | bytes accessed | tf_op | source)
XLA Modules:
  0.0 38.2 jit_solution(4927365975173337496)
XLA Ops:
  0.0 1.4 %copy.12.nlist_hbm = s32[16,4]{1,0:T(8,128)} copy(s32[16,4]{0,1:T(4,128)} %param.14) | data formatting | bytes 512 | tf_op args[3]
  1.4 1.3 %copy.13.flist_hbm = s32[16,8]{1,0:T(8,128)} copy(s32[16,8]{0,1:T(8,128)} %param.15) | data formatting | bytes 1024 | tf_op args[4]
  2.7 33.6 %h2_product.1 = bf16[16,64,256]{2,1,0:T(8,128)(2,1)} custom-call(bf16[16,64,256]{2,1,0:T(8,128)(2,1)} %charges_hbm.1, bf16[16,64,256]{2,1,0:T(8,128)(2,1)} %basis_hbm.1, bf16[16,4,256,256]{3,2,1,0:T(8,128)(2,1)} %near_hbm.1, s32[16,4]{1,0:T(8,128)} %copy.12.nlist_hbm, s32[16,8]{1,0:T(8,128)} %copy.13.flist_hbm, s32[16]{0:T(128)} %fcount_hbm.1, ...), custom_call_target="tpu_custom_call" | custom-call | tf_op jit(solution)/shard_map/h2_product/pallas_call | solution.py:377
  36.3 1.9 %copy.15 = bf16[16,64,256]{2,1,0:T(8,128)(2,1)} copy(bf16[16,64,256]{2,1,0:T(8,128)(2,1)} %h2_product.1) | data formatting | bytes 1048576

commit v2 on v1

--- a/solution.py
+++ b/solution.py
@@ -18,7 +18,8 @@
 NFAR = 8
 NNEAR = 4
 HALF = PAIRS // 2
-DEEP = NFAR * 128 + 256
+DEEP = NFAR * 128
+GROUP = 4
 offsets = (-3, -2, 2, 3)
 NT = (((1,), (1,)), ((), ()))
 
@@ -41,7 +42,8 @@
 
 
 TABLE = messages()
-COPIES = len(TABLE)
+WAVES = ((0, 1), (4, 5), (2, 3), (6, 7, 8, 9), (10, 13), (11, 12, 14, 15, 16, 17, 18, 19, 20, 21))
+WAVE_OF = {index: wave for wave, indices in enumerate(WAVES) for index in indices}
 
 
 def split(x):
@@ -67,12 +69,22 @@
     charges_hbm, basis_hbm, near_hbm, nlist_hbm, flist_hbm, fcount_hbm, coup_hbm, lt_hbm, dt_hbm, tt_hbm, lc_hbm,
     out_hbm,
     charges, basis, near, nlist, flist, fcount, coup, lt, dt, tt, lc,
-    skel, gup, deep, acc, wtab, wcat, ubd, tsend, rs, zsend, zrecv, ag, out,
+    skel, gup, gdn, deep, coupled, acc, wtab, wcat, ubd, tsend, rs, zsend, zrecv, ag, out,
     load_sem, near_sem, coup_sem, out_sem, skel_send, skel_recv, rs_send, rs_recv, z_send, z_recv, ag_send, ag_recv,
 ):
     l = lax.axis_index("leaf")
     j = lax.axis_index("list")
     x, y = j % SIDE, j // SIDE
+
+    barrier = pltpu.get_barrier_semaphore()
+
+    @pl.loop(1, LEAF)
+    def _(o):
+        pl.semaphore_signal(barrier, inc=1, device_id={"leaf": (l + o) % LEAF}, device_id_type=MESH)
+
+    @pl.loop(1, LIST)
+    def _(o):
+        pl.semaphore_signal(barrier, inc=1, device_id={"list": (j + o) % LIST}, device_id_type=MESH)
 
     loads = [
         pltpu.make_async_copy(charges_hbm, charges, load_sem.at[0]),
@@ -88,32 +100,33 @@
         pltpu.make_async_copy(lc_hbm.at[LEAF + l // 2], lc.at[1], load_sem.at[10]),
         pltpu.make_async_copy(lc_hbm.at[LEAF + LEAF // 2 + l // 4], lc.at[2], load_sem.at[11]),
     ]
-    for load in loads:
+
+    def near_copy(group):
+        leaves = pl.ds(group * GROUP, GROUP)
+        return pltpu.make_async_copy(near_hbm.at[leaves], near.at[leaves], near_sem.at[group])
+
+    coup_copy = pltpu.make_async_copy(coup_hbm, coup, coup_sem)
+
+    for load in loads[:7]:
         load.start()
-
-    def near_copy(c):
-        return pltpu.make_async_copy(near_hbm.at[c], near.at[c], near_sem.at[c])
-
-    def coup_copy(c):
-        return pltpu.make_async_copy(coup_hbm.at[c], coup.at[c], coup_sem.at[c])
-
-    def out_copy(c):
-        return pltpu.make_async_copy(out.at[c], out_hbm.at[c], out_sem.at[c])
-
-    barrier = pltpu.get_barrier_semaphore()
-
-    @pl.loop(1, LIST)
-    def _(o):
-        pl.semaphore_signal(barrier, inc=1, device_id={"list": (j + o) % LIST}, device_id_type=MESH)
-
-    @pl.loop(1, LEAF)
-    def _(o):
-        pl.semaphore_signal(barrier, inc=1, device_id={"leaf": (l + o) % LEAF}, device_id_type=MESH)
-
-    @pl.loop(0, LEAVES)
-    def _(c):
-        near_copy(c).start()
-        coup_copy(c).start()
+    for group in range(2):
+        near_copy(group).start()
+    for load in loads[7:]:
+        load.start()
+    for group in range(2, LEAVES // GROUP):
+        near_copy(group).start()
+    coup_copy.start()
+
+    loads[0].wait()
+    loads[1].wait()
+    for i in range(PAIRS):
+        both = lax.dot_general(
+            charges[2 * i : 2 * i + 2].reshape(2 * R, M),
+            basis[2 * i : 2 * i + 2].reshape(2 * K, M),
+            NT,
+            preferred_element_type=f32,
+        )
+        skel[j * PAIRS + i] = jnp.where(left_half((R, 128)), both[:R], both[R:]).astype(bf16)
 
     loads[2].wait()
     loads[3].wait()
@@ -123,19 +136,8 @@
     wide = left_half((LEAVES * K, 128))
     high32, low32 = g_high.astype(f32), g_low.astype(f32)
     gup[...] = jnp.where(wide, high32, low32).astype(bf16)
-    deep[:, :, NFAR * 128 : NFAR * 128 + 128] = g_high.reshape(LEAVES, K, 128)
-    deep[:, :, NFAR * 128 + 128 :] = jnp.where(wide, low32, 0.0).astype(bf16).reshape(LEAVES, K, 128)
-
-    loads[0].wait()
-    loads[1].wait()
-    for i in range(PAIRS):
-        both = lax.dot_general(
-            charges[2 * i : 2 * i + 2].reshape(2 * R, M),
-            basis[2 * i : 2 * i + 2].reshape(2 * K, M),
-            NT,
-            preferred_element_type=f32,
-        )
-        skel[j * PAIRS + i] = jnp.where(left_half((R, 128)), both[:R], both[R:]).astype(bf16)
+    gdn[:, :128] = g_high
+    gdn[:, 128:] = jnp.where(wide, low32, 0.0).astype(bf16)
 
     own = jnp.concatenate([skel[j * PAIRS + i] for i in range(PAIRS)], axis=1)
     term = jnp.dot(own, gup[...], preferred_element_type=f32)
@@ -145,6 +147,25 @@
         tsend[group] = jnp.where(left_half((8, 128)), rows[:8], rows[8:])
     rs[j] = tsend[y]
 
+    def near_group(group):
+        near_copy(group).wait()
+
+        @pl.loop(group * GROUP, group * GROUP + GROUP, step=2)
+        def _(first_leaf):
+            totals = []
+            for c in (first_leaf, first_leaf + 1):
+                total = lax.dot_general(charges[nlist[0, c]], near[c, 0], NT, preferred_element_type=f32)
+                for k in range(1, NNEAR):
+                    total += lax.dot_general(charges[nlist[k, c]], near[c, k], NT, preferred_element_type=f32)
+                totals.append(total)
+            for n, total in enumerate(totals):
+                acc[first_leaf + n] = total
+
+    for load in loads[4:7]:
+        load.wait()
+    near_group(0)
+    near_group(1)
+
     pl.semaphore_wait(barrier, LIST + LEAF - 2)
 
     def rs_copy(o):
@@ -152,8 +173,8 @@
         return pltpu.make_async_remote_copy(
             src_ref=tsend.at[peer // SIDE],
             dst_ref=rs.at[j],
-            send_sem=rs_send.at[o],
-            recv_sem=rs_recv.at[o],
+            send_sem=rs_send,
+            recv_sem=rs_recv,
             device_id={"list": peer},
             device_id_type=MESH,
         )
@@ -163,8 +184,8 @@
         return pltpu.make_async_remote_copy(
             src_ref=zsend.at[level_of(l, peer)],
             dst_ref=zrecv.at[l],
-            send_sem=z_send.at[o],
-            recv_sem=z_recv.at[o],
+            send_sem=z_send,
+            recv_sem=z_recv,
             device_id={"leaf": peer},
             device_id_type=MESH,
         )
@@ -173,8 +194,8 @@
         return pltpu.make_async_remote_copy(
             src_ref=ag.at[y],
             dst_ref=ag.at[y],
-            send_sem=ag_send.at[o],
-            recv_sem=ag_recv.at[o],
+            send_sem=ag_send,
+            recv_sem=ag_recv,
             device_id={"list": (y + o) % SIDE * SIDE + x},
             device_id_type=MESH,
         )
@@ -191,8 +212,8 @@
         return pltpu.make_async_remote_copy(
             src_ref=where,
             dst_ref=where,
-            send_sem=skel_send.at[half, index],
-            recv_sem=skel_recv.at[half, index],
+            send_sem=skel_send,
+            recv_sem=skel_recv.at[WAVE_OF[index]],
             device_id={"list": place(to)},
             device_id_type=MESH,
         )
@@ -202,10 +223,25 @@
             for half in (0, 1):
                 skel_copy(half, index).start()
 
+    def all_of(ref, count, send_sem, recv_sem):
+        part = ref.at[pl.ds(0, count)]
+        return pltpu.make_async_remote_copy(
+            src_ref=part,
+            dst_ref=part,
+            send_sem=send_sem,
+            recv_sem=recv_sem,
+            device_id={"list": (j + 1) % LIST},
+            device_id_type=MESH,
+        )
+
     def receive(*indices):
-        for index in indices:
-            for half in (0, 1):
-                skel_copy(half, index).wait_recv()
+        wave = WAVES.index(indices)
+        count = 2 * sum(TABLE[index][3] for index in indices)
+        all_of(skel, count, skel_send, skel_recv.at[wave]).wait_recv()
+
+    rs_all = all_of(rs, LIST - 1, rs_send, rs_recv)
+    z_all = all_of(zrecv, LEAF - 1, z_send, z_recv)
+    ag_all = all_of(ag, SIDE - 1, ag_send, ag_recv)
 
     @pl.loop(1, LIST)
     def _(o):
@@ -213,7 +249,7 @@
 
     send(0, 1, 4, 5)
 
-    for load in loads[4:]:
+    for load in loads[7:]:
         load.wait()
     first = tt[0]
     second = jnp.dot(first, tt[1], precision=lax.Precision.HIGHEST)
@@ -246,29 +282,14 @@
         ubd[:, 256 + 128 * n : 256 + 128 * n + 128] = low
     zrecv[l] = jnp.zeros((8, 128), f32)
 
-    def near_leaves(begin, end):
-        @pl.loop(begin, end)
-        def _(c):
-            near_copy(c).wait()
-            coup_copy(c).wait()
-            total = lax.dot_general(charges[nlist[c, 0]], near[c, 0], NT, preferred_element_type=f32)
-            for k in range(1, NNEAR):
-                total += lax.dot_general(charges[nlist[c, k]], near[c, k], NT, preferred_element_type=f32)
-            acc[c] = total
-            for k in range(NFAR):
-                matrix = coup[c, k]
-                deep[c, :, 128 * k : 128 * k + 128] = jnp.concatenate([matrix, matrix], axis=1)
-
-    near_leaves(0, 5)
+    near_group(2)
 
     receive(0, 1)
     send(2, 3, 6, 7, 8, 9)
     receive(4, 5)
     send(14, 15)
 
-    @pl.loop(1, LIST)
-    def _(o):
-        rs_copy(o).wait_recv()
+    rs_all.wait_recv()
 
     node = jnp.sum(rs[...], axis=0)
     high, low = split(node)
@@ -283,18 +304,25 @@
     def _(o):
         z_copy(o).start()
 
-    near_leaves(5, 10)
+    near_group(3)
+    coup_copy.wait()
+
+    @pl.loop(0, LEAVES, step=2)
+    def _(first_leaf):
+        for c in (first_leaf, first_leaf + 1):
+            for k in range(NFAR):
+                matrix = coup[c, k]
+                deep[c, :, 128 * k : 128 * k + 128] = jnp.concatenate([matrix, matrix], axis=1)
 
     receive(2, 3)
     send(10, 11, 12, 13)
     receive(6, 7, 8, 9)
     send(16, 17, 18, 19)
 
-    near_leaves(10, 14)
-
-    @pl.loop(1, LEAF)
-    def _(o):
-        z_copy(o).wait_recv()
+    receive(10, 13)
+    send(20, 21)
+
+    z_all.wait_recv()
 
     tops, bottoms = [], []
     narrow = left_half((8, 128))
@@ -311,13 +339,35 @@
     for o in range(1, SIDE):
         ag_copy(o).start()
 
-    receive(10, 13)
-    send(20, 21)
-
-    near_leaves(14, 16)
-
-    for o in range(1, SIDE):
-        ag_copy(o).wait_recv()
+    receive(11, 12, 14, 15, 16, 17, 18, 19, 20, 21)
+
+    lane = lax.broadcasted_iota(i32, (1, 128), 1) // 64
+    pair_mask = left_half((R, 128))
+
+    @pl.loop(0, PAIRS, step=2)
+    def _(first_pair):
+        results = []
+        for i in (first_pair, first_pair + 1):
+            rows = []
+            for c in (2 * i, 2 * i + 1):
+                pieces = []
+                for k in range(NFAR):
+                    source = flist[k, c]
+                    wanted = jnp.where(k < fcount[c], source % 2, 2)
+                    keep = jnp.where(lane == wanted, 1.0, 0.0).astype(bf16)
+                    pieces.append(skel[source // 2] * keep)
+                rows.append(jnp.concatenate(pieces, axis=1))
+            both = lax.dot_general(
+                jnp.concatenate(rows, axis=0),
+                deep[pl.ds(2 * i, 2)].reshape(2 * K, DEEP),
+                NT,
+                preferred_element_type=f32,
+            )
+            results.append(jnp.where(pair_mask, both[:R], both[R:]))
+        for n, result in enumerate(results):
+            coupled[first_pair + n] = result
+
+    ag_all.wait_recv()
     parts = []
     for group in range(SIDE):
         tile = ag[group]
@@ -333,45 +383,30 @@
         axis=1,
     )
 
-    receive(11, 12, 14, 15, 16, 17, 18, 19, 20, 21)
-
-    lane = lax.broadcasted_iota(i32, (1, 128), 1) // 64
-
-    @pl.loop(0, LEAVES)
-    def _(c):
-        pieces = []
-        for k in range(NFAR):
-            source = flist[c, k]
-            wanted = jnp.where(k < fcount[c], source % 2, 2)
-            keep = jnp.where(lane == wanted, 1.0, 0.0).astype(bf16)
-            pieces.append(skel[source // 2] * keep)
-        pieces.append(above)
-        coefficients = lax.dot_general(jnp.concatenate(pieces, axis=1), deep[c], NT, preferred_element_type=f32).astype(bf16)
-        far = jnp.dot(coefficients, basis[c], preferred_element_type=f32)
-        out[c] = (far + acc[c]).astype(bf16)
-        out_copy(c).start()
-
-    for index in range(COPIES):
-        for half in (0, 1):
-            skel_copy(half, index).wait_send()
-
-    @pl.loop(1, LIST)
-    def _(o):
-        rs_copy(o).wait_send()
-
-    @pl.loop(1, LEAF)
-    def _(o):
-        z_copy(o).wait_send()
-
-    for o in range(1, SIDE):
-        ag_copy(o).wait_send()
-
-    @pl.loop(0, LEAVES)
-    def _(c):
-        out_copy(c).wait()
-
-
-def on_device(*args):
+    for begin in range(0, PAIRS, 4):
+        values = []
+        for i in range(begin, begin + 4):
+            down_part = lax.dot_general(above, gdn[2 * K * i : 2 * K * i + 2 * K], NT, preferred_element_type=f32)
+            coefficients = coupled[i] + down_part
+            rows = jnp.concatenate(
+                [jnp.where(pair_mask, coefficients, 0.0), jnp.where(pair_mask, 0.0, coefficients)], axis=0
+            ).astype(bf16)
+            far = jnp.dot(rows, basis[2 * i : 2 * i + 2].reshape(2 * K, M), preferred_element_type=f32)
+            values.append((far + acc[2 * i : 2 * i + 2].reshape(2 * R, M)).astype(bf16))
+        for n, value in enumerate(values):
+            out[2 * (begin + n) : 2 * (begin + n) + 2] = value.reshape(2, R, M)
+        leaves = pl.ds(2 * begin, 8)
+        pltpu.make_async_copy(out.at[leaves], out_hbm.at[leaves], out_sem).start()
+
+    all_of(skel, (LIST - 1) * PAIRS, skel_send, skel_recv.at[0]).wait_send()
+    rs_all.wait_send()
+    z_all.wait_send()
+    ag_all.wait_send()
+    pltpu.make_async_copy(out, out_hbm, out_sem).wait()
+
+
+def on_device(charges, basis, near, near_list, far_list, *rest):
+    args = (charges, basis, near, near_list.T, far_list.T, *rest)
     anywhere = pl.BlockSpec(memory_space=pl.ANY)
     dma = pltpu.SemaphoreType.DMA
     return pl.pallas_call(
@@ -383,8 +418,8 @@
             pltpu.VMEM((LEAVES, R, M), bf16),
             pltpu.VMEM((LEAVES, K, M), bf16),
             pltpu.VMEM((LEAVES, NNEAR, M, M), bf16),
-            pltpu.SMEM((LEAVES, NNEAR), i32),
-            pltpu.SMEM((LEAVES, NFAR), i32),
+            pltpu.SMEM((NNEAR, LEAVES), i32),
+            pltpu.SMEM((NFAR, LEAVES), i32),
             pltpu.SMEM((LEAVES,), i32),
             pltpu.VMEM((LEAVES, NFAR, K, K), bf16),
             pltpu.VMEM((LEAVES, K, K), f32),
@@ -393,7 +428,9 @@
             pltpu.VMEM((3, 4, K, K), f32),
             pltpu.VMEM((LIST * PAIRS, R, 128), bf16),
             pltpu.VMEM((LEAVES * K, 128), bf16),
+            pltpu.VMEM((LEAVES * K, 256), bf16),
             pltpu.VMEM((LEAVES, K, DEEP), bf16),
+            pltpu.VMEM((PAIRS, R, 128), f32),
             pltpu.VMEM((LEAVES, R, M), f32),
             pltpu.VMEM((13, K, 128), f32),
             pltpu.VMEM((2 * K, LEAF * K), bf16),
@@ -405,17 +442,17 @@
             pltpu.VMEM((SIDE, 8, 128), f32),
             pltpu.VMEM((LEAVES, R, M), bf16),
             dma((12,)),
-            dma((LEAVES,)),
-            dma((LEAVES,)),
-            dma((LEAVES,)),
-            dma((2, COPIES)),
-            dma((2, COPIES)),
-            dma((LIST,)),
-            dma((LIST,)),
-            dma((LEAF,)),
-            dma((LEAF,)),
-            dma((SIDE,)),
-            dma((SIDE,)),
+            dma((LEAVES // GROUP,)),
+            dma(()),
+            dma(()),
+            dma(()),
+            dma((len(WAVES),)),
+            dma(()),
+            dma(()),
+            dma(()),
+            dma(()),
+            dma(()),
+            dma(()),
         ],
         compiler_params=pltpu.CompilerParams(collective_id=0, has_side_effects=True),
         name="h2_product",

time: 38.6 us -> 31.4 us (0.81)
  Pallas kernels: 33.6 us -> 29.2 us
  local copies, waits for them, and re-layouts: 4.58 us -> 1.88 us
    pallas_call x1, Pallas kernels: 33.6 us -> 29.2 us  [on_device(): pl.pallas_call(kernel, out_shape=jax.ShapeDtypeStruct((LEAVES, R, M), bf1...]
    unnamed x3 -> x1, local copies, waits for them, and re-layouts: 4.58 us -> 1.88 us
where the time goes in v2:
time: 31.4 us; the launch traced here: 31.1 us
  Pallas kernels  29.2 us (93%)
  local copies, waits for them, and re-layouts  1.88 us (6%)
    pallas_call x1, Pallas kernels, on_device(): pl.pallas_call(kernel, out_shape=jax.ShapeDtypeStruct((LEAVES, R, M), bf1...  29.2 us
    unnamed x1, local copies, waits for them, and re-layouts  1.88 us

profile of v2, /device:TPU:32, one launch (start us, length us, event | category | flops | bytes accessed | tf_op | source)
XLA Modules:
  0.0 31.1 jit_solution(7251826283025173713)
XLA Ops:
  0.0 29.2 %h2_product.1 = bf16[16,64,256]{2,1,0:T(8,128)(2,1)} custom-call(bf16[16,64,256]{2,1,0:T(8,128)(2,1)} %charges_hbm.1, bf16[16,64,256]{2,1,0:T(8,128)(2,1)} %basis_hbm.1, bf16[16,4,256,256]{3,2,1,0:T(8,128)(2,1)} %near_hbm.1, s32[4,16]{1,0:T(4,128)} %bitcast.3, s32[8,16]{1,0:T(8,128)} %bitcast.2, s32[16]{0:T(128)} %fcount_hbm.1, ...), custom_call_target="tpu_custom_call" | custom-call | tf_op jit(solution)/shard_map/h2_product/pallas_call | solution.py:412
  29.2 1.9 %copy.13 = bf16[16,64,256]{2,1,0:T(8,128)(2,1)} copy(bf16[16,64,256]{2,1,0:T(8,128)(2,1)} %h2_product.1) | data formatting | bytes 1048576
